TPU v7x, 256 devices: a whole 4x4x8 slice. The times are simulated.
256 devices in a mesh: ctx: 16 (over y, x), exp: 8 (over z), dp: 2 (over core).
Axes of the slice: x: 4, y: 4, z: 8, core: 2. Of those that a mesh axis runs over, the one named last changes fastest.
Arguments:
- residual: bfloat16 [2048, 4096], P('ctx', ('exp', 'dp')), may hold values from -6 to 6
- ssm_values: bfloat16 [2048, 4096], P('ctx', ('exp', 'dp')), may hold values from -6 to 6
- ssm_keys: bfloat16 [2048, 64], P('ctx'), may hold values from -6 to 6
- ssm_queries: bfloat16 [2048, 64], P('ctx'), may hold values from -0.015625 to 0.015625
- log_decay: float32 [2048, 64], P('ctx', ('exp', 'dp')), may hold values from -1 to 0, as said below
- expert_ids: int32 [2048, 2], P('ctx'), may hold values from 0 to 7, all different within a row; in each aligned block of 128 rows (0 to 127, 128 to 255, ...) at most 40 rows name the same one
- gate_probs: float32 [2048, 2], P('ctx'), may hold values from 0.2 to 1
- norm_gain: float32 [4096], P(('exp', 'dp')), may hold values from 0.5 to 1.5
- w_gate: bfloat16 [8, 4096, 8192], P('exp', None, ('ctx', 'dp')), may hold values from -0.09375 to 0.09375
- w_up: bfloat16 [8, 4096, 8192], P('exp', None, ('ctx', 'dp')), may hold values from -0.09375 to 0.09375
- w_down: bfloat16 [8, 4096, 8192], P('exp', None, ('ctx', 'dp')), may hold values from -0.0625 to 0.0625
- out_grad: bfloat16 [2048, 4096], P('ctx', ('exp', 'dp')), may hold values from -6 to 6
Outputs:
- grad_residual: bfloat16 [2048, 4096], P('ctx', ('exp', 'dp'))
- grad_values: bfloat16 [2048, 4096], P('ctx', ('exp', 'dp'))
- grad_keys: float32 [2048, 64], P('ctx')
- grad_queries: float32 [2048, 64], P('ctx')
- grad_decay: float32 [2048, 64], P('ctx', ('exp', 'dp'))
- grad_probs: float32 [2048, 2], P('ctx')
- grad_gain: float32 [4096], P(('exp', 'dp'))
- w_gate_grad: bfloat16 [8, 4096, 8192], P('exp', None, ('ctx', 'dp'))
- w_up_grad: bfloat16 [8, 4096, 8192], P('exp', None, ('ctx', 'dp'))
- w_down_grad: bfloat16 [8, 4096, 8192], P('exp', None, ('ctx', 'dp'))
Inputs may be any that keep to these rules, and one draw needn't show every extreme that they name: `expert_ids`: each token names two different experts; among the 128 tokens of one index of ctx (aligned blocks) no expert is named more than 40 times, a bound that some block reaches. `log_decay`: negative everywhere.
All inputs are finite; a program needn't handle non-finite values.
Results may differ from a plain program's by a relative error of at most 0.028.
Values may be sent and summed in bfloat16 or wider, within the bound.
No kernel may reach another device: no remote copies, remote signals or barrier semaphores. Data moves between devices by JAX's collectives and lax.ppermute only.
A program may use at most 128 MiB of HBM per device.

v0:
```python
import jax
import jax.numpy as jnp
from jax import lax
from jax.sharding import PartitionSpec as P

HIGH = lax.Precision.HIGHEST
EPS = 1e-05


def entering(x, axis, join, neutral):
    place = lax.axis_index(axis)
    gathered = jax.tree.map(
        lambda a, kind: lax.all_gather(a.astype(kind), axis), x, (jnp.bfloat16, jnp.bfloat16)
    )
    state = jax.tree.map(lambda a, e: jnp.zeros_like(a) + jnp.asarray(e, a.dtype), x, neutral)

    def entering_one(step, state):
        return join(
            state,
            jax.tree.map(
                lambda a, own: lax.dynamic_index_in_dim(a, step, 0, False).astype(own.dtype),
                gathered,
                x,
            ),
        )

    return lax.fori_loop(0, place, entering_one, state)


def carried_in(x, axis, join, neutral):
    count = lax.axis_size(axis)
    place = lax.axis_index(axis)
    ahead = count - 1 - place
    gathered = jax.tree.map(
        lambda a, kind: lax.all_gather(a.astype(kind), axis),
        x,
        jax.tree.map(lambda a: jnp.bfloat16 if a.dtype == jnp.float32 else a.dtype, x),
    )
    state = jax.tree.map(lambda a, e: jnp.zeros_like(a) + jnp.asarray(e, a.dtype), x, neutral)

    def carried_one(step, state):
        source = count - 1 - step
        return join(
            state,
            jax.tree.map(
                lambda a, own: lax.dynamic_index_in_dim(a, source, 0, False).astype(own.dtype),
                gathered,
                x,
            ),
        )

    return lax.fori_loop(0, ahead, carried_one, state)


def block_state(values, key_rows, log_decay):
    cumulative = jnp.cumsum(log_decay, axis=0)
    total_log = cumulative[-1]
    tail_decay = jnp.exp(total_log[None, :] - cumulative)
    weighted = tail_decay[:, :, None] * values
    state_local = jnp.einsum("shp,sn->hpn", weighted, key_rows, precision=HIGH)
    return (jnp.exp(total_log), state_local)


def block_output(values, key_rows, queries, log_decay, state_in):
    cumulative = jnp.cumsum(log_decay, axis=0)
    length = values.shape[0]
    row_index = lax.broadcasted_iota(jnp.int32, (length, length), 0)
    col_index = lax.broadcasted_iota(jnp.int32, (length, length), 1)
    causal = (row_index >= col_index)[None]
    cum_heads = cumulative.T
    log_gap = jnp.where(causal, cum_heads[:, :, None] - cum_heads[:, None, :], 0.0)
    decay_mat = jnp.where(causal, jnp.exp(log_gap), 0.0)
    scores = jnp.dot(queries, key_rows.T, precision=HIGH)
    inner_part = jnp.einsum("hts,shp->thp", decay_mat * scores[None], values, precision=HIGH)
    carried = jnp.einsum("tn,hpn->thp", queries, state_in, precision=HIGH)
    return inner_part + jnp.exp(cumulative)[:, :, None] * carried


def silu_parts(gate_act):
    sigmoid_val = jax.nn.sigmoid(gate_act)
    return (gate_act * sigmoid_val, sigmoid_val * (1.0 + gate_act * (1.0 - sigmoid_val)))


def route_slots(token_ids, expert_count):
    owners = token_ids.reshape(-1)
    onehot = (owners[:, None] == jnp.arange(expert_count, dtype=jnp.int32)[None, :]).astype(
        jnp.int32
    )
    rank_before = jnp.cumsum(onehot, axis=0) - onehot
    return (owners, jnp.sum(rank_before * onehot, axis=1))


def combine_states(earlier_part, later_part):
    return (
        earlier_part[0] * later_part[0],
        later_part[0][:, None, None] * earlier_part[1] + later_part[1],
    )


def arrange_rows(gathered, ctx_count, dp_count):
    capacity = gathered.shape[1]
    exp_count = gathered.shape[2]
    feat = gathered.shape[3]
    shaped = gathered.reshape(ctx_count, dp_count, capacity, exp_count, feat)
    return shaped.transpose(0, 2, 3, 1, 4).reshape(
        ctx_count * capacity, exp_count * dp_count * feat
    )


def arrange_sums(full_term, ctx_count, dp_count, exp_count, capacity):
    feat = full_term.shape[1] // (exp_count * dp_count)
    shaped = full_term.reshape(ctx_count, capacity, exp_count, dp_count, feat)
    return shaped.transpose(0, 3, 1, 2, 4).reshape(
        ctx_count * dp_count * capacity, exp_count * feat
    )


def per_device(
    residual,
    ssm_values,
    ssm_keys,
    ssm_queries,
    log_decay,
    expert_ids,
    gate_probs,
    norm_gain,
    w_gate,
    w_up,
    w_down,
    out_grad,
):
    tokens = residual.shape[0]
    feat = residual.shape[1]
    heads_here = log_decay.shape[1]
    head_size = feat // heads_here
    model_width = w_gate.shape[1]
    ctx_count = lax.axis_size("ctx")
    exp_count = lax.axis_size("exp")
    dp_count = lax.axis_size("dp")
    expert_count = w_gate.shape[0] * exp_count
    capacity = 5 * tokens // (2 * expert_count)
    block_vals = ssm_values.astype(jnp.float32).reshape(tokens, heads_here, head_size)
    block_keys = ssm_keys.astype(jnp.float32)
    block_queries = ssm_queries.astype(jnp.float32)
    (decay_total, state_local), state_pull = jax.vjp(block_state, block_vals, block_keys, log_decay)
    neutral = (jnp.ones_like(decay_total), jnp.zeros_like(state_local))
    state_in = entering((decay_total, state_local), "ctx", combine_states, neutral)[1]
    mixer_out, output_pull = jax.vjp(
        block_output, block_vals, block_keys, block_queries, log_decay, state_in
    )
    hidden = (residual.astype(jnp.float32) + mixer_out.reshape(tokens, feat)).astype(jnp.bfloat16)
    hidden_f = hidden.astype(jnp.float32)
    square_sum = lax.psum(jnp.sum(hidden_f * hidden_f, axis=1), ("exp", "dp"))
    inv_rms = lax.rsqrt(square_sum / model_width + EPS)[:, None]
    normed = (hidden_f * inv_rms * norm_gain[None, :]).astype(jnp.bfloat16)
    owners, slot_index = route_slots(expert_ids, expert_count)
    pair_rows = jnp.repeat(normed, 2, axis=0)
    dout_rows = jnp.repeat(out_grad, 2, axis=0)
    pair_prob = gate_probs.reshape(-1)
    pair_cot = (pair_prob[:, None] * dout_rows.astype(jnp.float32)).astype(jnp.bfloat16)
    empty = jnp.zeros((expert_count, capacity, feat), jnp.bfloat16)
    send_rows = empty.at[owners, slot_index].set(pair_rows).reshape(expert_count, capacity, 1, feat)
    got_rows = lax.all_to_all(send_rows, "exp", split_axis=0, concat_axis=2, tiled=True)
    all_rows = lax.all_gather(got_rows, ("ctx", "dp"), axis=0, tiled=True)
    rows_flat = arrange_rows(all_rows, ctx_count, dp_count)
    act_gate = jnp.dot(rows_flat, w_gate[0], preferred_element_type=jnp.float32)
    act_up = jnp.dot(rows_flat, w_up[0], preferred_element_type=jnp.float32)
    swish_val, swish_slope = silu_parts(act_gate)
    hidden_act = (swish_val * act_up).astype(jnp.bfloat16)
    full_out = lax.dot_general(
        hidden_act, w_down[0], (((1,), (1,)), ((), ())), preferred_element_type=jnp.float32
    )
    out_total = lax.psum_scatter(
        arrange_sums(full_out, ctx_count, dp_count, exp_count, capacity).astype(jnp.bfloat16),
        ("ctx", "dp"),
        scatter_dimension=0,
        tiled=True,
    )
    expert_out = out_total.reshape(1, capacity, exp_count, feat)
    back_out = lax.all_to_all(expert_out, "exp", split_axis=2, concat_axis=0, tiled=True).reshape(
        expert_count, capacity, feat
    )
    out_pairs = back_out[owners, slot_index]
    probs_part = jnp.einsum(
        "kd,kd->k", out_pairs, dout_rows, preferred_element_type=jnp.float32
    ).reshape(tokens, 2)
    grad_probs = lax.psum(probs_part, ("exp", "dp"))
    send_cot = empty.at[owners, slot_index].set(pair_cot).reshape(expert_count, capacity, 1, feat)
    got_cot = lax.all_to_all(send_cot, "exp", split_axis=0, concat_axis=2, tiled=True)
    all_cot = lax.all_gather(got_cot, ("ctx", "dp"), axis=0, tiled=True)
    cot_flat = arrange_rows(all_cot, ctx_count, dp_count)
    grad_act = jnp.dot(cot_flat, w_down[0], preferred_element_type=jnp.float32)
    grad_gate = (grad_act * act_up * swish_slope).astype(jnp.bfloat16)
    grad_up = (grad_act * swish_val).astype(jnp.bfloat16)
    full_back = lax.dot_general(
        grad_gate, w_gate[0], (((1,), (1,)), ((), ())), preferred_element_type=jnp.float32
    ) + lax.dot_general(
        grad_up, w_up[0], (((1,), (1,)), ((), ())), preferred_element_type=jnp.float32
    )
    back_total = lax.psum_scatter(
        arrange_sums(full_back, ctx_count, dp_count, exp_count, capacity).astype(jnp.bfloat16),
        ("ctx", "dp"),
        scatter_dimension=0,
        tiled=True,
    )
    pair_back = back_total.reshape(1, capacity, exp_count, feat)
    back_in = lax.all_to_all(pair_back, "exp", split_axis=2, concat_axis=0, tiled=True).reshape(
        expert_count, capacity, feat
    )
    grad_normed = (
        back_in[owners, slot_index].astype(jnp.float32).reshape(tokens, 2, feat).sum(axis=1)
    )
    w_gate_grad = jnp.dot(rows_flat.T, grad_gate, preferred_element_type=jnp.float32).astype(
        jnp.bfloat16
    )[None]
    w_up_grad = jnp.dot(rows_flat.T, grad_up, preferred_element_type=jnp.float32).astype(
        jnp.bfloat16
    )[None]
    w_down_grad = jnp.dot(cot_flat.T, hidden_act, preferred_element_type=jnp.float32).astype(
        jnp.bfloat16
    )[None]
    scaled = grad_normed * norm_gain[None, :]
    inner_sum = lax.psum(jnp.sum(hidden_f * scaled, axis=1), ("exp", "dp"))
    projection = (inner_sum / model_width)[:, None]
    grad_hidden = (
        out_grad.astype(jnp.float32) + inv_rms * scaled - hidden_f * inv_rms**3 * projection
    )
    gain_part = jnp.sum(grad_normed * hidden_f * inv_rms, axis=0)
    grad_gain = lax.psum(gain_part, "ctx")
    grad_mixer = grad_hidden.reshape(tokens, heads_here, head_size)
    vals_first, keys_first, queries_part, decay_first, carry_cot = output_pull(grad_mixer)
    grad_state = carried_in((decay_total, carry_cot), "ctx", combine_states, neutral)[1]
    grad_total = jnp.sum(grad_state * state_in, axis=(1, 2))
    vals_second, keys_second, decay_second = state_pull((grad_total, grad_state))
    grad_keys, grad_queries = (
        lax.psum((keys_first + keys_second).astype(jnp.bfloat16), ("exp", "dp")).astype(
            jnp.float32
        ),
        lax.psum(queries_part.astype(jnp.bfloat16), ("exp", "dp")).astype(jnp.float32),
    )
    grad_residual = grad_hidden.astype(jnp.bfloat16)
    grad_values = (vals_first + vals_second).reshape(tokens, feat).astype(jnp.bfloat16)
    grad_decay = decay_first + decay_second
    return (
        grad_residual,
        grad_values,
        grad_keys,
        grad_queries,
        grad_decay,
        grad_probs,
        grad_gain,
        w_gate_grad,
        w_up_grad,
        w_down_grad,
    )


def solution(mesh):
    return jax.shard_map(
        per_device,
        mesh=mesh,
        in_specs=(
            P("ctx", ("exp", "dp")),
            P("ctx", ("exp", "dp")),
            P("ctx", None),
            P("ctx", None),
            P("ctx", ("exp", "dp")),
            P("ctx", None),
            P("ctx", None),
            P(("exp", "dp")),
            P("exp", None, ("ctx", "dp")),
            P("exp", None, ("ctx", "dp")),
            P("exp", None, ("ctx", "dp")),
            P("ctx", ("exp", "dp")),
        ),
        out_specs=(
            P("ctx", ("exp", "dp")),
            P("ctx", ("exp", "dp")),
            P("ctx", None),
            P("ctx", None),
            P("ctx", ("exp", "dp")),
            P("ctx", None),
            P(("exp", "dp")),
            P("exp", None, ("ctx", "dp")),
            P("exp", None, ("ctx", "dp")),
            P("exp", None, ("ctx", "dp")),
        ),
        check_vma=False,
    )
```

profile of v0, /device:TPU:2, one launch (start us, length us, event | category | flops | bytes accessed | tf_op | source)
XLA Modules:
  0.0 650.5 jit_solution(5369685150378966095)
XLA Ops:
  11.6 13.2 %scatter_fusion = bf16[8,40,256]{2,1,0:T(8,128)(2,1)S(1)} fusion(bf16[8,40,256]{2,1,0:T(8,128)(2,1)S(1)} %broadcast_in_dim.73.clone.1, s32[256]{0:T(256)S(1)} %bitcast.193, bf16[256,256]{1,0:T(8,128)(2,1)S(1)} %fusion.19), kind=kCustom, calls=%fused_computation.2 | custom fusion | bytes 395264 | tf_op jit(solution)/shard_map/scatter | solution.py:188
  24.9 18.0 %all_to_all.66 = bf16[8,40,1,256]{3,1,2,0:T(8,128)(2,1)S(1)} all-to-all(bf16[8,40,1,256]{3,1,2,0:T(8,128)(2,1)S(1)} %bitcast.200), channel_id=1, replica_groups=mesh['ctx'=16,'exp'=8,'dp'=2] {'exp'}, dimensions={0} | all-to-all | bytes 327680 | tf_op jit(solution)/shard_map/all_to_all | solution.py:189
  44.6 20.7 %all-gather.4 = bf16[16,1,4]{2,1,0:T(2,128)(2,1)S(1)} all-gather(bf16[1,1,4]{2,1,0:T(2,128)(2,1)S(1)} %get-tuple-element.299), channel_id=1, replica_groups=mesh['ctx'=16,'exp'=8,'dp'=2] {'ctx'}, dimensions={0}, use_global_device_ids=true | all-gather | bytes 136 | tf_op jit(solution)/shard_map/all_gather | solution.py:13
  67.0 27.6 %all-gather = bf16[64,64,64]{2,1,0:T(8,128)(2,1)} all-gather(bf16[4,64,64]{2,1,0:T(8,128)(2,1)S(1)} %convolution_convert_fusion.4), channel_id=2, replica_groups=mesh['ctx'=16,'exp'=8,'dp'=2] {'ctx'}, dimensions={0}, use_global_device_ids=true | all-gather | bytes 557056 | tf_op jit(solution)/shard_map/all_gather | solution.py:13
  96.7 23.5 %psum.42 = f32[128]{0:T(128)S(1)} all-reduce(f32[128]{0:T(128)S(1)} %get-tuple-element.291), channel_id=1, replica_groups=mesh['ctx'=16,'exp'=8,'dp'=2] {'exp','dp'}, use_global_device_ids=true, to_apply=%region_4.5 | all-reduce | flops 128 | bytes 1024 | tf_op jit(solution)/shard_map/psum | solution.py:153
  121.1 13.2 %scatter_fusion.1 = bf16[8,40,256]{2,1,0:T(8,128)(2,1)S(1)} fusion(bf16[8,40,256]{2,1,0:T(8,128)(2,1)S(1)} %broadcast_in_dim.73.clone, s32[256]{0:T(256)S(1)} %bitcast.194, bf16[256,256]{1,0:T(8,128)(2,1)S(1)} %reshape.273), kind=kCustom, calls=%fused_computation.3 | custom fusion | bytes 395264 | tf_op jit(solution)/shard_map/scatter | solution.py:162
  134.3 12.5 %all_to_all.67 = bf16[8,40,1,256]{3,1,2,0:T(8,128)(2,1)S(1)} all-to-all(bf16[8,40,1,256]{3,1,2,0:T(8,128)(2,1)S(1)} %bitcast.199), channel_id=1, replica_groups=mesh['ctx'=16,'exp'=8,'dp'=2] {'exp'}, dimensions={0} | all-to-all | bytes 327680 | tf_op jit(solution)/shard_map/all_to_all | solution.py:163
  148.1 13.0 %copy.164 = bf16[16,40,8,2,256]{4,3,2,1,0:T(2,128)(2,1)} copy(bf16[16,40,8,2,256]{4,2,1,3,0:T(8,128)(2,1)} %bitcast.203) | data formatting | bytes 10485760 | tf_op jit(solution)/shard_map/transpose | solution.py:105
  161.1 9.6 %reshape.236 = bf16[640,4096]{1,0:T(8,128)(2,1)} reshape(bf16[16,40,8,2,256]{4,3,2,1,0:T(2,128)(2,1)} %copy.164) | data formatting | bytes 10485760 | tf_op jit(solution)/shard_map/reshape | solution.py:105
  170.7 35.8 %all-gather.10.cloned.1.call-done = bf16[32,40,8,1,256]{4,2,3,1,0:T(8,128)(2,1)} async-done(((bf16[1,40,8,1,256]{4,2,3,1,0:T(8,128)(2,1)}), bf16[32,40,8,1,256]{4,2,3,1,0:T(8,128)(2,1)}) %all-gather.10.cloned.1.call-update) | async-done | bytes 5242896 | tf_op jit(solution)/shard_map/all_gather | solution.py:164
  206.6 13.0 %copy.167 = bf16[16,40,8,2,256]{4,3,2,1,0:T(2,128)(2,1)} copy(bf16[16,40,8,2,256]{4,2,1,3,0:T(8,128)(2,1)} %bitcast.204) | data formatting | bytes 10485760 | tf_op jit(solution)/shard_map/transpose | solution.py:105
  219.6 9.6 %reshape.240 = bf16[640,4096]{1,0:T(8,128)(2,1)} reshape(bf16[16,40,8,2,256]{4,3,2,1,0:T(2,128)(2,1)} %copy.167) | data formatting | bytes 10485760 | tf_op jit(solution)/shard_map/reshape | solution.py:105
  229.2 4.2 fusion.10
  235.5 2.4 multiply_convert_fusion
  239.6 2.3 copy.176
  241.9 4.6 copy.191
  249.8 3.8 add_convert_fusion
  253.6 9.6 %convert_element_type.165 = bf16[16,40,8,2,256]{4,3,2,1,0:T(2,128)(2,1)} reshape(bf16[640,4096]{1,0:T(8,128)(2,1)} %add_convert_fusion) | data formatting | bytes 10485760 | tf_op jit(solution)/shard_map/convert_element_type | solution.py:201
  263.2 3.6 copy.168
  266.8 4.5 copy.189
  272.3 5.9 fusion.2
  278.2 60.3 %reduce-scatter.5.cloned.1.call-done = bf16[40,2048]{1,0:T(8,128)(2,1)} async-done(((bf16[1280,2048]{1,0:T(8,128)(2,1)}), bf16[40,2048]{1,0:T(8,128)(2,1)}) %reduce-scatter.5.cloned.1.call-update) | async-done | bytes 163856 | tf_op jit(solution)/shard_map/reduce_scatter | solution.py:173
  340.1 7.0 %all-to-all-start.3 = ((bf16[1,40,8,256]{3,1,0,2:T(8,128)(2,1)}), bf16[1,40,8,256]{3,1,0,2:T(8,128)(2,1)S(1)}, u32[]{:S(2)}, u32[]{:S(2)}) async-start(bf16[1,40,8,256]{3,1,0,2:T(8,128)(2,1)} %copy.177), calls=%async_computation.5 | async-start | bytes 327680 | tf_op jit(solution)/shard_map/all_to_all | solution.py:180
  347.2 5.7 fusion
  352.9 81.2 %reduce-scatter.3.cloned.1.call-done = bf16[40,2048]{1,0:T(8,128)(2,1)} async-done(((bf16[1280,2048]{1,0:T(8,128)(2,1)}), bf16[40,2048]{1,0:T(8,128)(2,1)}) %reduce-scatter.3.cloned.1.call-update) | async-done | bytes 163856 | tf_op jit(solution)/shard_map/reduce_scatter | solution.py:200
  435.8 7.2 %all-to-all-start.2 = ((bf16[1,40,8,256]{3,1,0,2:T(8,128)(2,1)}), bf16[1,40,8,256]{3,1,0,2:T(8,128)(2,1)S(1)}, u32[]{:S(2)}, u32[]{:S(2)}) async-start(bf16[1,40,8,256]{3,1,0,2:T(8,128)(2,1)} %copy.169), calls=%async_computation.3 | async-start | bytes 327680 | tf_op jit(solution)/shard_map/all_to_all | solution.py:207
  443.0 5.7 fusion.1
  454.6 46.5 %all-reduce.1 = (f32[128]{0:T(128)S(1)}, f32[128,2]{1,0:T(8,128)S(1)}) all-reduce(f32[128]{0:T(128)S(1)} %get-tuple-element.264, f32[128,2]{1,0:T(8,128)S(1)} %reshape.247), channel_id=1, replica_groups=mesh['ctx'=16,'exp'=8,'dp'=2] {'exp','dp'}, use_global_device_ids=true, to_apply=%region_13.14 | all-reduce | flops 384 | bytes 3072 | tf_op jit(solution)/shard_map/psum | solution.py:223
  502.6 25.1 %all-gather.3 = bf16[64,64,64]{2,1,0:T(8,128)(2,1)} all-gather(bf16[4,64,64]{2,1,0:T(8,128)(2,1)S(1)} %convolution_convert_fusion.3), channel_id=5, replica_groups=mesh['ctx'=16,'exp'=8,'dp'=2] {'ctx'}, dimensions={0}, use_global_device_ids=true | all-gather | bytes 557056 | tf_op jit(solution)/shard_map/all_gather | solution.py:35
  527.7 22.9 %while.27 = (s32[]{:T(128)}, f32[4,64,64]{2,1,0:T(8,128)S(1)}, s32[]{:T(128)}, bf16[16,4]{1,0:T(8,128)(2,1)}, bf16[16,4,64,64]{3,2,1,0:T(8,128)(2,1)}, /*index=5*/s32[]{:T(128)}, s32[]{:T(128)}, s32[]{:T(128)}, s32[]{:T(128)}) while((s32[]{:T(128)}, f32[4,64,64]{2,1,0:T(8,128)S(1)}, s32[]{:T(128)}, bf16[16,4]{1,0:T(8,128)(2,1)}, ...), condition=%wide.region_15.16_spmd, body=%wide.region_14.15_spmd.sunk | while | flops 49162 | bytes 164035 | solution.py:52
  550.9 39.5 %psum.47 = f32[256]{0:T(256)} all-reduce(f32[256]{0:T(256)S(1)} %get-tuple-element.263), channel_id=1, replica_groups=mesh['ctx'=16,'exp'=8,'dp'=2] {'ctx'}, use_global_device_ids=true, to_apply=%region_30.31 | all-reduce | flops 256 | bytes 2048 | tf_op jit(solution)/shard_map/psum | solution.py:229
  593.7 45.7 %all-reduce.2 = (bf16[128,64]{0,1:T(8,128)(2,1)S(1)}, bf16[128,64]{0,1:T(8,128)(2,1)S(1)}) all-reduce(bf16[128,64]{0,1:T(8,128)(2,1)S(1)} %fusion.16, bf16[128,64]{0,1:T(8,128)(2,1)S(1)} %fusion.17), channel_id=1, replica_groups=mesh['ctx'=16,'exp'=8,'dp'=2] {'exp','dp'}, use_global_device_ids=true, to_apply=%region_17.18 | all-reduce | flops 16384 | bytes 65536 | tf_op jit(solution)/shard_map/psum | solution.py:236
  (171 shorter events, 61.8 us)
Async XLA Ops:
  7.2 222.0 %copy-start = (bf16[1,4096,256]{2,1,0:T(8,128)(2,1)S(1)}, bf16[1,4096,256]{2,1,0:T(8,128)(2,1)}, u32[]{:S(2)}) copy-start(bf16[1,4096,256]{2,1,0:T(8,128)(2,1)} %param.26) | copy-start | bytes 6291460
  7.2 59.6 %copy-start.13 = (bf16[128,64]{0,1:T(8,128)(2,1)S(1)}, bf16[128,64]{0,1:T(8,128)(2,1)}, u32[]{:S(2)}) copy-start(bf16[128,64]{0,1:T(8,128)(2,1)} %param.18) | copy-start | bytes 49156
  7.2 87.4 %copy-start.12 = (bf16[128,64]{0,1:T(8,128)(2,1)S(1)}, bf16[128,64]{0,1:T(8,128)(2,1)}, u32[]{:S(2)}) copy-start(bf16[128,64]{0,1:T(8,128)(2,1)} %param.19) | copy-start | bytes 49156
  7.2 89.4 %copy-start.16 = (bf16[128,256]{1,0:T(8,128)(2,1)S(1)}, bf16[128,256]{1,0:T(8,128)(2,1)}, u32[]{:S(2)}) copy-start(bf16[128,256]{1,0:T(8,128)(2,1)} %param.16) | copy-start | bytes 196612
  7.2 113.6 %copy-start.17 = (f32[256]{0:T(256)S(1)}, f32[256]{0:T(256)}, u32[]{:S(2)}) copy-start(f32[256]{0:T(256)} %param.23) | copy-start | bytes 3076
  7.2 140.9 %all-gather.8.cloned.1.call-start = ((), (), s32[]{:S(2)}) async-start(), calls=%async_computation.8 | async-start | bytes 5406720 | tf_op jit(solution)/shard_map/all_gather | solution.py:190
  43.6 163.0 %all-gather.10.cloned.1.call-start = ((), (), s32[]{:S(2)}) async-start(), calls=%async_computation.9 | async-start | bytes 5406720 | tf_op jit(solution)/shard_map/all_gather | solution.py:164
  66.4 67.9 %copy-start.19 = (f32[4,128]{1,0:T(4,128)}, f32[4,128]{1,0:T(4,128)S(1)}, u32[]{:S(2)}) copy-start(f32[4,128]{1,0:T(4,128)S(1)} %copy.150) | copy-start | bytes 6148
  94.8 39.5 %copy-start.14 = (f32[128,128]{1,0:T(8,128)}, f32[128,128]{1,0:T(8,128)S(1)}, u32[]{:S(2)}) copy-start(f32[128,128]{1,0:T(8,128)S(1)} %fusion.65) | copy-start | bytes 196612
  95.8 38.5 %copy-start.18 = (bf16[16,4]{1,0:T(8,128)(2,1)}, bf16[16,4]{1,0:T(8,128)(2,1)S(1)}, u32[]{:S(2)}) copy-start(bf16[16,4]{1,0:T(8,128)(2,1)S(1)} %get-tuple-element.437) | copy-start | bytes 388
  147.5 191.0 %reduce-scatter.5.cloned.1.call-start = ((), (), s32[]{:S(2)}) async-start(), calls=%async_computation.7 | async-start | bytes 5406720 | tf_op jit(solution)/shard_map/reduce_scatter | solution.py:173
  229.2 4.2 copy-start.2
  229.2 4.7 copy-start.3
  233.9 1.6 copy-start.5
  238.0 3.9 copy-start.9
  246.6 1.6 copy-start.4
  246.6 187.5 %reduce-scatter.3.cloned.1.call-start = ((), (), s32[]{:S(2)}) async-start(), calls=%async_computation.6 | async-start | bytes 5406720 | tf_op jit(solution)/shard_map/reduce_scatter | solution.py:200
  248.2 1.6 copy-start.6
  248.2 1.6 copy-start.7
  271.3 1.0 copy-start.10
  340.1 95.7 %all-to-all-start.3 = ((bf16[1,40,8,256]{3,1,0,2:T(8,128)(2,1)}), bf16[1,40,8,256]{3,1,0,2:T(8,128)(2,1)S(1)}, u32[]{:S(2)}, u32[]{:S(2)}) async-start(bf16[1,40,8,256]{3,1,0,2:T(8,128)(2,1)} %copy.177), calls=%async_computation.5 | async-start | bytes 327680 | tf_op jit(solution)/shard_map/all_to_all | solution.py:180
  347.2 95.8 %copy-start.8 = (bf16[640,256]{1,0:T(8,128)(2,1)S(1)}, bf16[640,256]{1,0:T(8,128)(2,1)}, u32[]{:S(2)}) copy-start(bf16[640,256]{1,0:T(8,128)(2,1)} %get-tuple-element.297) | copy-start | bytes 983044
  435.8 16.6 %all-to-all-start.2 = ((bf16[1,40,8,256]{3,1,0,2:T(8,128)(2,1)}), bf16[1,40,8,256]{3,1,0,2:T(8,128)(2,1)S(1)}, u32[]{:S(2)}, u32[]{:S(2)}) async-start(bf16[1,40,8,256]{3,1,0,2:T(8,128)(2,1)} %copy.169), calls=%async_computation.3 | async-start | bytes 327680 | tf_op jit(solution)/shard_map/all_to_all | solution.py:207
  443.0 58.1 %copy-start.11 = (bf16[128,256]{1,0:T(8,128)(2,1)S(1)}, bf16[128,256]{1,0:T(8,128)(2,1)}, u32[]{:S(2)}) copy-start(bf16[128,256]{1,0:T(8,128)(2,1)} %param.27) | copy-start | bytes 196612
  443.0 58.1 %copy-start.21 = (f32[128]{0:T(128)S(1)}, f32[128]{0:T(128)}, u32[]{:S(2)}) copy-start(f32[128]{0:T(128)} %get-tuple-element.300) | copy-start | bytes 1540
  448.7 142.3 %copy-start.15 = (f32[128,128]{1,0:T(8,128)S(1)}, f32[128,128]{1,0:T(8,128)}, u32[]{:S(2)}) copy-start(f32[128,128]{1,0:T(8,128)} %copy-done.14) | copy-start | bytes 196612
  448.7 142.3 %copy-start.20 = (f32[4,128]{1,0:T(4,128)S(1)}, f32[4,128]{1,0:T(4,128)}, u32[]{:S(2)}) copy-start(f32[4,128]{1,0:T(4,128)} %copy-done.19) | copy-start | bytes 6148
  452.4 191.4 %copy-start.1 = (bf16[1,4096,256]{2,1,0:T(8,128)(2,1)S(1)}, bf16[1,4096,256]{2,1,0:T(8,128)(2,1)}, u32[]{:S(2)}) copy-start(bf16[1,4096,256]{2,1,0:T(8,128)(2,1)} %param.26) | copy-start | bytes 6291460
Sparse Core Ops, SparseCore 0:
  43.7 49.1 all-gather.7
  147.6 58.8 all-gather.9
  246.7 91.7 reduce-scatter.4
  342.4 91.7 reduce-scatter.2
where the time goes:
time: 657 us; the launch traced here: 650 us
  blocking collectives  259 us (39%)
  waiting for transfers between devices  179 us (27%)
  local copies, waits for them, and re-layouts  116 us (18%)
  matrix products  35.9 us (5%)
  other arithmetic  30.4 us (5%)
  starting transfers between devices  15.3 us (2%)
  between operations  14.5 us (2%)
    reduce_scatter x1, waiting for transfers between devices, per_device(): lax.psum_scatter(arrange_sums(full_back, ctx_count, dp_count, exp_count,...  81.2 us
    reduce_scatter x1, waiting for transfers between devices, per_device(): lax.psum_scatter(arrange_sums(full_out, ctx_count, dp_count, exp_count, c...  60.3 us
    all_gather x2, blocking collectives, entering(): lax.all_gather(a.astype(kind), axis)  48.3 us
    psum x1, blocking collectives, per_device(): inner_sum = lax.psum(jnp.sum(hidden_f * scaled, axis=1), ('exp', 'dp'))  46.5 us
    psum x1, blocking collectives, per_device(): lax.psum((keys_first + keys_second).astype(jnp.bfloat16), ('exp', 'dp'))  45.7 us
    psum x1, blocking collectives, per_device(): grad_gain = lax.psum(gain_part, 'ctx')  39.5 us
    all_gather x1, waiting for transfers between devices, per_device(): all_rows = lax.all_gather(got_rows, ('ctx', 'dp'), axis=0, tiled=True)  35.8 us
    transpose x2, local copies, waits for them, and re-layouts, arrange_rows(): shaped.transpose(0, 2, 3, 1, 4)  26 us
  transfers between devices with their start and end apart: 6, of which 4 were waited for; matrix products, arithmetic and copies ran while one was open for 13% of the time, Pallas kernels for 0%

commit v1 on v0

--- a/solution.py
+++ b/solution.py
@@ -5,6 +5,23 @@
 
 HIGH = lax.Precision.HIGHEST
 EPS = 1e-05
+
+
+def detail_table(incoming_x):
+    world_n = lax.axis_size("ctx")
+
+    def form_tiles(b_now, frame_out):
+        if frame_out >= world_n:
+            return b_now
+        w_next = range(world_n)
+        y2 = map(lambda w: (w, w ^ frame_out), w_next)
+        back = list(y2)
+        part_now = lax.ppermute(b_now, "ctx", back)
+        a_next = form_tiles(b_now + part_now, 2 * frame_out)
+        return a_next
+
+    current_arr = form_tiles(incoming_x, 1)
+    return current_arr
 
 
 def entering(x, axis, join, neutral):
@@ -226,7 +243,7 @@
         out_grad.astype(jnp.float32) + inv_rms * scaled - hidden_f * inv_rms**3 * projection
     )
     gain_part = jnp.sum(grad_normed * hidden_f * inv_rms, axis=0)
-    grad_gain = lax.psum(gain_part, "ctx")
+    grad_gain = detail_table(gain_part)
     grad_mixer = grad_hidden.reshape(tokens, heads_here, head_size)
     vals_first, keys_first, queries_part, decay_first, carry_cot = output_pull(grad_mixer)
     grad_state = carried_in((decay_total, carry_cot), "ctx", combine_states, neutral)[1]

time: 657 us -> 632 us (0.962)
  blocking collectives: 259 us -> 220 us
  waiting for transfers between devices: 179 us -> 188 us
    psum x1 -> x0, blocking collectives: 39.5 us -> none  [per_device(): grad_gain = lax.psum(gain_part, 'ctx')]
    ppermute x0 -> x4, waiting for transfers between devices: none -> 8.6 us  [form_tiles(): part_now = lax.ppermute(b_now, 'ctx', back)]
  transfers between devices with their start and end apart: 6 -> 10, of which waited for: 4 -> 6; matrix products, arithmetic and copies ran while one was open for 13% -> 15% of each run, Pallas kernels for 0% -> 0%
where the time goes in v1:
time: 632 us; the launch traced here: 624 us
  blocking collectives  220 us (35%)
  waiting for transfers between devices  188 us (30%)
  local copies, waits for them, and re-layouts  116 us (18%)
  matrix products  35.9 us (6%)
  other arithmetic  31 us (5%)
  starting transfers between devices  18.4 us (3%)
  between operations  14.6 us (2%)
    reduce_scatter x1, waiting for transfers between devices, per_device(): lax.psum_scatter(arrange_sums(full_back, ctx_count, dp_count, exp_count,...  81.2 us
    reduce_scatter x1, waiting for transfers between devices, per_device(): lax.psum_scatter(arrange_sums(full_out, ctx_count, dp_count, exp_count, c...  60.4 us
    all_gather x2, blocking collectives, entering(): lax.all_gather(a.astype(kind), axis)  48.3 us
    psum x1, blocking collectives, per_device(): inner_sum = lax.psum(jnp.sum(hidden_f * scaled, axis=1), ('exp', 'dp'))  46.5 us
    psum x1, blocking collectives, per_device(): lax.psum((keys_first + keys_second).astype(jnp.bfloat16), ('exp', 'dp'))  46 us
    all_gather x1, waiting for transfers between devices, per_device(): all_rows = lax.all_gather(got_rows, ('ctx', 'dp'), axis=0, tiled=True)  36.2 us
    transpose x2, local copies, waits for them, and re-layouts, arrange_rows(): shaped.transpose(0, 2, 3, 1, 4)  26 us
    all_gather x1, blocking collectives, carried_in(): lax.all_gather(a.astype(kind), axis)  25 us
  transfers between devices with their start and end apart: 10, of which 6 were waited for; matrix products, arithmetic and copies ran while one was open for 15% of the time, Pallas kernels for 0%

profile of v1, /device:TPU:2, one launch (start us, length us, event | category | flops | bytes accessed | tf_op | source)
XLA Modules:
  0.0 624.2 jit_solution(6892878452611891266)
XLA Ops:
  11.6 13.2 %scatter_fusion = bf16[8,40,256]{2,1,0:T(8,128)(2,1)S(1)} fusion(bf16[8,40,256]{2,1,0:T(8,128)(2,1)S(1)} %broadcast_in_dim.73.clone.1, s32[256]{0:T(256)S(1)} %bitcast.193, bf16[256,256]{1,0:T(8,128)(2,1)S(1)} %fusion.19), kind=kCustom, calls=%fused_computation.2 | custom fusion | bytes 395264 | tf_op jit(solution)/shard_map/scatter | solution.py:205
  24.9 18.0 %all_to_all.66 = bf16[8,40,1,256]{3,1,2,0:T(8,128)(2,1)S(1)} all-to-all(bf16[8,40,1,256]{3,1,2,0:T(8,128)(2,1)S(1)} %bitcast.200), channel_id=1, replica_groups=mesh['ctx'=16,'exp'=8,'dp'=2] {'exp'}, dimensions={0} | all-to-all | bytes 327680 | tf_op jit(solution)/shard_map/all_to_all | solution.py:206
  44.6 20.7 %all-gather.4 = bf16[16,1,4]{2,1,0:T(2,128)(2,1)S(1)} all-gather(bf16[1,1,4]{2,1,0:T(2,128)(2,1)S(1)} %get-tuple-element.299), channel_id=1, replica_groups=mesh['ctx'=16,'exp'=8,'dp'=2] {'ctx'}, dimensions={0}, use_global_device_ids=true | all-gather | bytes 136 | tf_op jit(solution)/shard_map/all_gather | solution.py:30
  67.0 27.6 %all-gather = bf16[64,64,64]{2,1,0:T(8,128)(2,1)} all-gather(bf16[4,64,64]{2,1,0:T(8,128)(2,1)S(1)} %convolution_convert_fusion.4), channel_id=2, replica_groups=mesh['ctx'=16,'exp'=8,'dp'=2] {'ctx'}, dimensions={0}, use_global_device_ids=true | all-gather | bytes 557056 | tf_op jit(solution)/shard_map/all_gather | solution.py:30
  96.7 23.5 %psum.35 = f32[128]{0:T(128)S(1)} all-reduce(f32[128]{0:T(128)S(1)} %get-tuple-element.291), channel_id=1, replica_groups=mesh['ctx'=16,'exp'=8,'dp'=2] {'exp','dp'}, use_global_device_ids=true, to_apply=%region_4.5 | all-reduce | flops 128 | bytes 1024 | tf_op jit(solution)/shard_map/psum | solution.py:170
  121.1 13.2 %scatter_fusion.1 = bf16[8,40,256]{2,1,0:T(8,128)(2,1)S(1)} fusion(bf16[8,40,256]{2,1,0:T(8,128)(2,1)S(1)} %broadcast_in_dim.73.clone, s32[256]{0:T(256)S(1)} %bitcast.194, bf16[256,256]{1,0:T(8,128)(2,1)S(1)} %reshape.273), kind=kCustom, calls=%fused_computation.3 | custom fusion | bytes 395264 | tf_op jit(solution)/shard_map/scatter | solution.py:179
  134.3 12.5 %all_to_all.67 = bf16[8,40,1,256]{3,1,2,0:T(8,128)(2,1)S(1)} all-to-all(bf16[8,40,1,256]{3,1,2,0:T(8,128)(2,1)S(1)} %bitcast.199), channel_id=1, replica_groups=mesh['ctx'=16,'exp'=8,'dp'=2] {'exp'}, dimensions={0} | all-to-all | bytes 327680 | tf_op jit(solution)/shard_map/all_to_all | solution.py:180
  147.8 13.0 %copy.164 = bf16[16,40,8,2,256]{4,3,2,1,0:T(2,128)(2,1)} copy(bf16[16,40,8,2,256]{4,2,1,3,0:T(8,128)(2,1)} %bitcast.203) | data formatting | bytes 10485760 | tf_op jit(solution)/shard_map/transpose | solution.py:122
  160.8 9.7 %reshape.236 = bf16[640,4096]{1,0:T(8,128)(2,1)} reshape(bf16[16,40,8,2,256]{4,3,2,1,0:T(2,128)(2,1)} %copy.164) | data formatting | bytes 10485760 | tf_op jit(solution)/shard_map/reshape | solution.py:122
  170.4 36.2 %all-gather.10.cloned.1.call-done = bf16[32,40,8,1,256]{4,2,3,1,0:T(8,128)(2,1)} async-done(((bf16[1,40,8,1,256]{4,2,3,1,0:T(8,128)(2,1)}), bf16[32,40,8,1,256]{4,2,3,1,0:T(8,128)(2,1)}) %all-gather.10.cloned.1.call-update) | async-done | bytes 5242896 | tf_op jit(solution)/shard_map/all_gather | solution.py:181
  206.6 13.0 %copy.167 = bf16[16,40,8,2,256]{4,3,2,1,0:T(2,128)(2,1)} copy(bf16[16,40,8,2,256]{4,2,1,3,0:T(8,128)(2,1)} %bitcast.204) | data formatting | bytes 10485760 | tf_op jit(solution)/shard_map/transpose | solution.py:122
  219.6 9.8 %reshape.240 = bf16[640,4096]{1,0:T(8,128)(2,1)} reshape(bf16[16,40,8,2,256]{4,3,2,1,0:T(2,128)(2,1)} %copy.167) | data formatting | bytes 10485760 | tf_op jit(solution)/shard_map/reshape | solution.py:122
  229.5 4.2 fusion.10
  241.9 4.6 copy.191
  249.8 3.8 add_convert_fusion
  253.6 9.6 %convert_element_type.165 = bf16[16,40,8,2,256]{4,3,2,1,0:T(2,128)(2,1)} reshape(bf16[640,4096]{1,0:T(8,128)(2,1)} %add_convert_fusion) | data formatting | bytes 10485760 | tf_op jit(solution)/shard_map/convert_element_type | solution.py:218
  263.2 3.6 copy.168
  266.8 4.5 copy.189
  272.3 5.9 fusion.2
  278.2 60.4 %reduce-scatter.5.cloned.1.call-done = bf16[40,2048]{1,0:T(8,128)(2,1)} async-done(((bf16[1280,2048]{1,0:T(8,128)(2,1)}), bf16[40,2048]{1,0:T(8,128)(2,1)}) %reduce-scatter.5.cloned.1.call-update) | async-done | bytes 163856 | tf_op jit(solution)/shard_map/reduce_scatter | solution.py:190
  340.2 7.0 %all-to-all-start.3 = ((bf16[1,40,8,256]{3,1,0,2:T(8,128)(2,1)}), bf16[1,40,8,256]{3,1,0,2:T(8,128)(2,1)S(1)}, u32[]{:S(2)}, u32[]{:S(2)}) async-start(bf16[1,40,8,256]{3,1,0,2:T(8,128)(2,1)} %copy.177), calls=%async_computation.5 | async-start | bytes 327680 | tf_op jit(solution)/shard_map/all_to_all | solution.py:197
  347.2 5.7 fusion
  352.9 81.2 %reduce-scatter.3.cloned.1.call-done = bf16[40,2048]{1,0:T(8,128)(2,1)} async-done(((bf16[1280,2048]{1,0:T(8,128)(2,1)}), bf16[40,2048]{1,0:T(8,128)(2,1)}) %reduce-scatter.3.cloned.1.call-update) | async-done | bytes 163856 | tf_op jit(solution)/shard_map/reduce_scatter | solution.py:217
  435.8 7.3 %all-to-all-start.2 = ((bf16[1,40,8,256]{3,1,0,2:T(8,128)(2,1)}), bf16[1,40,8,256]{3,1,0,2:T(8,128)(2,1)S(1)}, u32[]{:S(2)}, u32[]{:S(2)}) async-start(bf16[1,40,8,256]{3,1,0,2:T(8,128)(2,1)} %copy.169), calls=%async_computation.3 | async-start | bytes 327680 | tf_op jit(solution)/shard_map/all_to_all | solution.py:224
  443.1 5.7 fusion.1
  454.7 46.5 %all-reduce.1 = (f32[128]{0:T(128)S(1)}, f32[128,2]{1,0:T(8,128)S(1)}) all-reduce(f32[128]{0:T(128)S(1)} %get-tuple-element.264, f32[128,2]{1,0:T(8,128)S(1)} %reshape.247), channel_id=1, replica_groups=mesh['ctx'=16,'exp'=8,'dp'=2] {'exp','dp'}, use_global_device_ids=true, to_apply=%region_13.14 | all-reduce | flops 384 | bytes 3072 | tf_op jit(solution)/shard_map/psum | solution.py:240
  502.6 25.0 %all-gather.3 = bf16[64,64,64]{2,1,0:T(8,128)(2,1)} all-gather(bf16[4,64,64]{2,1,0:T(8,128)(2,1)S(1)} %convolution_convert_fusion.3), channel_id=5, replica_groups=mesh['ctx'=16,'exp'=8,'dp'=2] {'ctx'}, dimensions={0}, use_global_device_ids=true | all-gather | bytes 557056 | tf_op jit(solution)/shard_map/all_gather | solution.py:52
  527.6 22.9 %while.27 = (s32[]{:T(128)}, f32[4,64,64]{2,1,0:T(8,128)S(1)}, s32[]{:T(128)}, bf16[16,4]{1,0:T(8,128)(2,1)}, bf16[16,4,64,64]{3,2,1,0:T(8,128)(2,1)}, /*index=5*/s32[]{:T(128)}, s32[]{:T(128)}, s32[]{:T(128)}, s32[]{:T(128)}) while((s32[]{:T(128)}, f32[4,64,64]{2,1,0:T(8,128)S(1)}, s32[]{:T(128)}, bf16[16,4]{1,0:T(8,128)(2,1)}, ...), condition=%wide.region_15.16_spmd, body=%wide.region_14.15_spmd.sunk | while | flops 49162 | bytes 164035 | solution.py:69
  550.9 3.6 collective-permute-start
  556.6 5.0 collective-permute-done.1
  561.6 3.6 collective-permute-done.2
  565.2 46.0 %all-reduce.2 = (bf16[128,64]{0,1:T(8,128)(2,1)S(1)}, bf16[128,64]{0,1:T(8,128)(2,1)S(1)}) all-reduce(bf16[128,64]{0,1:T(8,128)(2,1)S(1)} %fusion.16, bf16[128,64]{0,1:T(8,128)(2,1)S(1)} %fusion.17), channel_id=1, replica_groups=mesh['ctx'=16,'exp'=8,'dp'=2] {'exp','dp'}, use_global_device_ids=true, to_apply=%region_17.18 | all-reduce | flops 16384 | bytes 65536 | tf_op jit(solution)/shard_map/psum | solution.py:253
  (182 shorter events, 66.7 us)
Async XLA Ops:
  7.2 222.2 %copy-start = (bf16[1,4096,256]{2,1,0:T(8,128)(2,1)S(1)}, bf16[1,4096,256]{2,1,0:T(8,128)(2,1)}, u32[]{:S(2)}) copy-start(bf16[1,4096,256]{2,1,0:T(8,128)(2,1)} %param.26) | copy-start | bytes 6291460
  7.2 59.6 %copy-start.13 = (bf16[128,64]{0,1:T(8,128)(2,1)S(1)}, bf16[128,64]{0,1:T(8,128)(2,1)}, u32[]{:S(2)}) copy-start(bf16[128,64]{0,1:T(8,128)(2,1)} %param.18) | copy-start | bytes 49156
  7.2 87.4 %copy-start.12 = (bf16[128,64]{0,1:T(8,128)(2,1)S(1)}, bf16[128,64]{0,1:T(8,128)(2,1)}, u32[]{:S(2)}) copy-start(bf16[128,64]{0,1:T(8,128)(2,1)} %param.19) | copy-start | bytes 49156
  7.2 89.4 %copy-start.16 = (bf16[128,256]{1,0:T(8,128)(2,1)S(1)}, bf16[128,256]{1,0:T(8,128)(2,1)}, u32[]{:S(2)}) copy-start(bf16[128,256]{1,0:T(8,128)(2,1)} %param.16) | copy-start | bytes 196612
  7.2 113.6 %copy-start.17 = (f32[256]{0:T(256)S(1)}, f32[256]{0:T(256)}, u32[]{:S(2)}) copy-start(f32[256]{0:T(256)} %param.23) | copy-start | bytes 3076
  7.2 140.5 %all-gather.8.cloned.1.call-start = ((), (), s32[]{:S(2)}) async-start(), calls=%async_computation.8 | async-start | bytes 5406720 | tf_op jit(solution)/shard_map/all_gather | solution.py:207
  43.6 163.0 %all-gather.10.cloned.1.call-start = ((), (), s32[]{:S(2)}) async-start(), calls=%async_computation.9 | async-start | bytes 5406720 | tf_op jit(solution)/shard_map/all_gather | solution.py:181
  66.4 67.9 %copy-start.19 = (f32[4,128]{1,0:T(4,128)}, f32[4,128]{1,0:T(4,128)S(1)}, u32[]{:S(2)}) copy-start(f32[4,128]{1,0:T(4,128)S(1)} %copy.150) | copy-start | bytes 6148
  94.8 39.5 %copy-start.14 = (f32[128,128]{1,0:T(8,128)}, f32[128,128]{1,0:T(8,128)S(1)}, u32[]{:S(2)}) copy-start(f32[128,128]{1,0:T(8,128)S(1)} %fusion.65) | copy-start | bytes 196612
  95.8 38.5 %copy-start.18 = (bf16[16,4]{1,0:T(8,128)(2,1)}, bf16[16,4]{1,0:T(8,128)(2,1)S(1)}, u32[]{:S(2)}) copy-start(bf16[16,4]{1,0:T(8,128)(2,1)S(1)} %get-tuple-element.441) | copy-start | bytes 388
  147.5 191.0 %reduce-scatter.5.cloned.1.call-start = ((), (), s32[]{:S(2)}) async-start(), calls=%async_computation.7 | async-start | bytes 5406720 | tf_op jit(solution)/shard_map/reduce_scatter | solution.py:190
  229.4 4.2 copy-start.2
  229.4 4.7 copy-start.3
  234.1 1.6 copy-start.5
  238.2 3.8 copy-start.9
  246.6 1.6 copy-start.4
  246.6 187.5 %reduce-scatter.3.cloned.1.call-start = ((), (), s32[]{:S(2)}) async-start(), calls=%async_computation.6 | async-start | bytes 5406720 | tf_op jit(solution)/shard_map/reduce_scatter | solution.py:217
  248.2 1.6 copy-start.6
  248.2 1.6 copy-start.7
  271.3 1.0 copy-start.10
  340.2 95.6 %all-to-all-start.3 = ((bf16[1,40,8,256]{3,1,0,2:T(8,128)(2,1)}), bf16[1,40,8,256]{3,1,0,2:T(8,128)(2,1)S(1)}, u32[]{:S(2)}, u32[]{:S(2)}) async-start(bf16[1,40,8,256]{3,1,0,2:T(8,128)(2,1)} %copy.177), calls=%async_computation.5 | async-start | bytes 327680 | tf_op jit(solution)/shard_map/all_to_all | solution.py:197
  347.2 95.8 %copy-start.8 = (bf16[640,256]{1,0:T(8,128)(2,1)S(1)}, bf16[640,256]{1,0:T(8,128)(2,1)}, u32[]{:S(2)}) copy-start(bf16[640,256]{1,0:T(8,128)(2,1)} %get-tuple-element.297) | copy-start | bytes 983044
  435.8 16.6 %all-to-all-start.2 = ((bf16[1,40,8,256]{3,1,0,2:T(8,128)(2,1)}), bf16[1,40,8,256]{3,1,0,2:T(8,128)(2,1)S(1)}, u32[]{:S(2)}, u32[]{:S(2)}) async-start(bf16[1,40,8,256]{3,1,0,2:T(8,128)(2,1)} %copy.169), calls=%async_computation.3 | async-start | bytes 327680 | tf_op jit(solution)/shard_map/all_to_all | solution.py:224
  443.0 58.1 %copy-start.11 = (bf16[128,256]{1,0:T(8,128)(2,1)S(1)}, bf16[128,256]{1,0:T(8,128)(2,1)}, u32[]{:S(2)}) copy-start(bf16[128,256]{1,0:T(8,128)(2,1)} %param.27) | copy-start | bytes 196612
  443.1 58.1 %copy-start.21 = (f32[128]{0:T(128)S(1)}, f32[128]{0:T(128)}, u32[]{:S(2)}) copy-start(f32[128]{0:T(128)} %get-tuple-element.300) | copy-start | bytes 1540
  448.8 105.7 %copy-start.15 = (f32[128,128]{1,0:T(8,128)S(1)}, f32[128,128]{1,0:T(8,128)}, u32[]{:S(2)}) copy-start(f32[128,128]{1,0:T(8,128)} %copy-done.14) | copy-start | bytes 196612
  448.8 105.7 %copy-start.20 = (f32[4,128]{1,0:T(4,128)S(1)}, f32[4,128]{1,0:T(4,128)}, u32[]{:S(2)}) copy-start(f32[4,128]{1,0:T(4,128)} %copy-done.19) | copy-start | bytes 6148
  452.4 165.0 %copy-start.1 = (bf16[1,4096,256]{2,1,0:T(8,128)(2,1)S(1)}, bf16[1,4096,256]{2,1,0:T(8,128)(2,1)}, u32[]{:S(2)}) copy-start(bf16[1,4096,256]{2,1,0:T(8,128)(2,1)} %param.26) | copy-start | bytes 6291460
  550.9 5.5 collective-permute-start
  556.5 5.2 collective-permute-start.1
  561.6 3.6 collective-permute-start.2
  565.2 51.6 %collective-permute-start.3 = (f32[256]{0:T(256)S(1)}, f32[256]{0:T(256)S(1)}, u32[]{:S(2)}, u32[]{:S(2)}) collective-permute-start(f32[256]{0:T(256)S(1)} %add.141), channel_id=1, source_target_pairs={{0,128},{16,144},{32,160},{48,176},{64,192},{80,208},{96,224},{112... | collective-permute-start | bytes 3080 | tf_op jit(solution)/shard_map/ppermute | solution.py:19
Sparse Core Ops, SparseCore 0:
  43.7 49.1 all-gather.7
  147.6 58.9 all-gather.9
  246.7 91.7 reduce-scatter.4
  342.4 91.6 reduce-scatter.2
